TPU v7x, 256 devices: a whole 4x4x8 slice. The times are simulated.
256 devices in a mesh: pair: 32 (over y, x, core), occ: 8 (over z).
Axes of the slice: x: 4, y: 4, z: 8, core: 2. Of those that a mesh axis runs over, the one named last changes fastest.
Arguments:
- half_ints: bfloat16 [8, 12288, 6144], P('occ', 'pair'), may hold values from -6 to 6
- pair_coef: bfloat16 [512, 12288], P('occ'), may hold values from -0.078125 to 0.078125
- mo_virtual: bfloat16 [5632, 6144], P('pair'), may hold values from -0.078125 to 0.078125
- screen: int32 [192], replicated, may hold values 0 or 1
- slot_block: int32 [192], replicated, may hold values from 0 to 191, each once
Outputs:
- mo_block: bfloat16 [5632, 8, 512], P('pair', 'occ')
Inputs may be any that keep to these rules, and one draw needn't show every extreme that they name: `screen`: 1 where the pair block survives screening, 0 where it is dropped. `slot_block`: each logical pair block stands in exactly one storage slot; index k of pair holds slots k * 6 to k * 6 + 5.
All inputs are finite; a program needn't handle non-finite values.
Results may differ from a plain program's by a relative error of at most 0.0049.
Values may be sent and summed in bfloat16 or wider, within the bound.
No kernel may reach another device: no remote copies, remote signals or barrier semaphores. Data moves between devices by JAX's collectives and lax.ppermute only.
A program may use at most 128 MiB of HBM per device.

v0:
```python
import jax
import jax.numpy as jnp
from jax import lax
from jax.sharding import PartitionSpec as P


def shards(half_ints, pair_coef, mo_virtual, screen, slot_block):
    coef_all = lax.all_gather(pair_coef, "occ", axis=0, tiled=True)
    occ_width = coef_all.shape[0]
    block_count = screen.shape[0]
    block_width = coef_all.shape[1] // block_count
    masked_coef = (
        coef_all.reshape(occ_width, block_count, block_width)
        * screen.astype(jnp.bfloat16)[None, :, None]
    )
    selected = jnp.take(masked_coef, slot_block, axis=1).reshape(
        occ_width, block_count * block_width
    )
    local_pairs = half_ints.shape[1]
    own_index = lax.axis_index("pair")
    local_cols = lax.dynamic_slice_in_dim(selected, own_index * local_pairs, local_pairs, 1)
    summed_pairs = lax.psum_scatter(
        jnp.einsum("jq,iqn->nij", local_cols, half_ints, preferred_element_type=jnp.float32),
        "pair",
        scatter_dimension=0,
        tiled=True,
    )
    occ_pair = summed_pairs.astype(jnp.bfloat16)
    item_width = occ_pair.shape[1] * occ_pair.shape[2]
    virt_count = mo_virtual.shape[0]
    block_part = lax.all_gather(occ_pair, "pair", axis=0, tiled=True)
    flat_rows = block_part.reshape(block_part.shape[0], item_width)
    folded = jnp.dot(mo_virtual, flat_rows, preferred_element_type=jnp.float32)
    return folded.reshape(virt_count, occ_pair.shape[1], occ_pair.shape[2]).astype(jnp.bfloat16)


def solution(mesh):
    placed = (P("occ", "pair", None), P("occ", None), P("pair", None), P(), P())
    return jax.shard_map(
        shards, mesh=mesh, in_specs=placed, out_specs=P("pair", "occ", None), check_vma=False
    )
```

profile of v0, /device:TPU:1, one launch (start us, length us, event | category | flops | bytes accessed | tf_op | source)
XLA Modules:
  0.0 1388.3 jit_solution(8234210186869820136)
XLA Ops:
  6.5 0.0 copy-start
  6.5 0.0 all-gather.3.cloned.1.call-start
  6.5 0.7 all-gather.3.cloned.1.call-update
  7.3 0.0 all-gather.5.cloned.1.call-start
  7.3 0.7 convert_element_type.15
  8.0 0.7 compare_and_fusion
  8.7 0.1 broadcast_in_dim.17
  8.8 0.1 broadcast_in_dim.18
  8.9 0.1 dynamic-slice.2
  9.0 1.3 dynamic-slice
  10.9 0.7 compare_select_fusion
  11.6 134.8 %all-gather.3.cloned.1.call-done = bf16[512,12288]{1,0:T(8,128)(2,1)} async-done(((bf16[64,12288]{1,0:T(8,128)(2,1)}), bf16[512,12288]{1,0:T(8,128)(2,1)}) %all-gather.3.cloned.1.call-update) | async-done | bytes 12582928 | tf_op jit(solution)/shard_map/all_gather | solution.py:8
  146.4 16.6 %copy.7 = bf16[512,12288]{0,1:T(8,128)(2,1)} copy(bf16[512,12288]{1,0:T(8,128)(2,1)} %all-gather.3.cloned.1.call-done) | data formatting | bytes 25165824 | tf_op jit(solution)/shard_map/all_gather | solution.py:8
  163.0 10.6 broadcast_multiply_fusion
  173.6 12.8 gather_fusion
  186.5 10.5 convolution_bitcast_fusion
  196.9 27.0 %copy.8 = f32[6144,1,512]{2,1,0:T(1,128)} copy(f32[6144,1,512]{0,2,1:T(8,128)} %convolution_bitcast_fusion) | data formatting | bytes 25165824 | tf_op jit(solution)/shard_map/jq,iqn->nij/transpose | solution.py:23
  224.0 1093.3 %all-reduce.2 = bf16[6144,1,512]{2,1,0:T(2,128)(2,1)} all-reduce(f32[6144,1,512]{2,1,0:T(1,128)} %copy.8), channel_id=2, replica_groups=mesh['pair'=32,'occ'=8] {'pair'}, use_global_device_ids=true, to_apply=%region_0.1.clone | all-reduce | flops 3145728 | bytes 18874368
  1317.3 1.4 dynamic-slice_convert_fusion
  1318.7 0.7 copy.9
  1319.4 0.0 all-gather.5.cloned.1.call-update
  1319.4 57.3 %all-gather.5.cloned.1.call-done = bf16[6144,1,512]{2,0,1:T(8,128)(2,1)} async-done(((bf16[192,1,512]{2,0,1:T(8,128)(2,1)}), bf16[6144,1,512]{2,0,1:T(8,128)(2,1)}) %all-gather.5.cloned.1.call-update) | async-done | bytes 6291472 | tf_op jit(solution)/shard_map/all_gather | solution.py:31
  1376.7 0.0 copy-done
  1376.7 4.7 fusion.6
  (1 shorter events, 0.0 us)
Async XLA Ops:
  6.5 1370.2 %copy-start = (bf16[176,6144]{1,0:T(8,128)(2,1)S(1)}, bf16[176,6144]{1,0:T(8,128)(2,1)}, u32[]{:S(2)}) copy-start(bf16[176,6144]{1,0:T(8,128)(2,1)} %param.7) | copy-start | bytes 6488068
  6.5 139.9 %all-gather.3.cloned.1.call-start = ((), (), s32[]{:S(2)}) async-start(), calls=%async_computation | async-start | bytes 14155776 | tf_op jit(solution)/shard_map/all_gather | solution.py:8
  7.3 1369.5 %all-gather.5.cloned.1.call-start = ((), (), s32[]{:S(2)}) async-start(), calls=%async_computation.1 | async-start | bytes 6488064 | tf_op jit(solution)/shard_map/all_gather | solution.py:31
Sparse Core Ops, SparseCore 0:
  9.1 137.2 all-gather.2
  1319.6 57.1 all-gather.4
where the time goes:
time: 1390 us
  blocking collectives  1090 us (78%)
  waiting for transfers between devices  193 us (14%)
  local copies, waits for them, and re-layouts  60.1 us (4%)
  matrix products  15.2 us (1%)
  between operations  14.1 us (1%)
    unnamed x1, blocking collectives  1090 us
    all_gather x1, waiting for transfers between devices, shards(): coef_all = lax.all_gather(pair_coef, 'occ', axis=0, tiled=True)  135 us
    all_gather x1, waiting for transfers between devices, shards(): block_part = lax.all_gather(occ_pair, 'pair', axis=0, tiled=True)  57.3 us
  transfers between devices with their start and end apart: 2, of which 2 were waited for; matrix products, arithmetic and copies ran while one was open for 0% of the time, Pallas kernels for 0%

commit v1 on v0

--- a/solution.py
+++ b/solution.py
@@ -3,9 +3,16 @@
 from jax import lax
 from jax.sharding import PartitionSpec as P
 
+turn_object = lambda arr_in, mesh_name: jnp.concatenate(
+    jax.lax.all_to_all(
+        jnp.stack([arr_in for _ in range(jax.lax.axis_size(mesh_name))], 0), mesh_name, 0, 0
+    ),
+    0,
+)
+
 
 def shards(half_ints, pair_coef, mo_virtual, screen, slot_block):
-    coef_all = lax.all_gather(pair_coef, "occ", axis=0, tiled=True)
+    coef_all = turn_object(pair_coef, "occ")
     occ_width = coef_all.shape[0]
     block_count = screen.shape[0]
     block_width = coef_all.shape[1] // block_count

time: 1390 us -> 1590 us (1.14)
  waiting for transfers between devices: 193 us -> 331 us
  local copies, waits for them, and re-layouts: 60.1 us -> 112 us
    all_to_all x0 -> x1, waiting for transfers between devices: none -> 276 us  [jax.lax.all_to_all(jnp.stack([arr_in for _ in range(jax.lax.axis_size(mes...]
    all_gather x1 -> x0, waiting for transfers between devices: 135 us -> none  [shards(): coef_all = lax.all_gather(pair_coef, 'occ', axis=0, tiled=True)]
    another operation x0 -> x3, local copies, waits for them, and re-layouts: none -> 68.9 us  [the longest x2 61.2 us: shards(): coef_all.reshape(occ_width, block_count, block_width)]
    all_gather x1 -> x0, local copies, waits for them, and re-layouts: 16.6 us -> none  [shards(): coef_all = lax.all_gather(pair_coef, 'occ', axis=0, tiled=True)]
where the time goes in v1:
time: 1590 us; the launch traced here: 1580 us
  blocking collectives  1090 us (69%)
  waiting for transfers between devices  331 us (21%)
  local copies, waits for them, and re-layouts  112 us (7%)
    unnamed x1, blocking collectives  1090 us
    all_to_all x1, waiting for transfers between devices, jax.lax.all_to_all(jnp.stack([arr_in for _ in range(jax.lax.axis_size(mes...  276 us
    another operation x2, local copies, waits for them, and re-layouts, shards(): coef_all.reshape(occ_width, block_count, block_width)  61.2 us
    all_gather x1, waiting for transfers between devices, shards(): block_part = lax.all_gather(occ_pair, 'pair', axis=0, tiled=True)  55 us
  transfers between devices with their start and end apart: 2, of which 2 were waited for; matrix products, arithmetic and copies ran while one was open for 0% of the time, Pallas kernels for 0%

profile of v1, /device:TPU:1, one launch (start us, length us, event | category | flops | bytes accessed | tf_op | source)
XLA Modules:
  0.0 1584.8 jit_solution(17412149255229692608)
XLA Ops:
  6.5 0.0 copy-start
  6.5 7.7 stack.2
  14.3 0.0 copy-start.2
  14.3 0.0 copy-start.1
  14.3 0.0 copy-start.3
  14.3 9.1 all-to-all-start
  23.4 0.0 all-gather.2.cloned.1.call-start
  23.5 0.0 copy-done.2
  23.5 0.0 copy-done.1
  23.5 0.1 broadcast_in_dim.17
  23.6 0.1 broadcast_in_dim.18
  23.7 0.1 dynamic-slice.2
  23.8 0.0 copy-done.3
  23.8 0.6 dynamic-slice
  25.1 275.7 %all-to-all-done = bf16[8,64,12288]{2,1,0:T(8,128)(2,1)} async-done(((bf16[8,64,12288]{2,1,0:T(8,128)(2,1)}), bf16[8,64,12288]{2,1,0:T(8,128)(2,1)}, u32[]{:S(2)}, u32[]{:S(2)}) %all-to-all-start) | async-done | bytes 12582944 | tf_op jit(solution)/shard_map/all_to_all | solution.py:7
  300.7 34.4 %reshape_reshape.3 = bf16[512,192,64]{2,1,0:T(8,128)(2,1)} reshape(bf16[8,64,12288]{2,1,0:T(8,128)(2,1)} %all-to-all-done) | data formatting | bytes 25165824 | tf_op jit(solution)/shard_map/reshape;reshape | solution.py:20
  335.1 26.8 %copy.7 = bf16[512,192,64]{0,2,1:T(8,128)(2,1)} copy(bf16[512,192,64]{2,1,0:T(8,128)(2,1)} %reshape_reshape.3) | data formatting | bytes 25165824 | tf_op jit(solution)/shard_map/reshape;reshape | solution.py:20
  361.9 10.7 broadcast_multiply_fusion
  372.6 12.8 gather_fusion
  385.4 10.5 convolution_bitcast_fusion
  395.9 27.0 %copy.8 = f32[6144,1,512]{2,1,0:T(1,128)} copy(f32[6144,1,512]{0,2,1:T(8,128)} %convolution_bitcast_fusion) | data formatting | bytes 25165824 | tf_op jit(solution)/shard_map/jq,iqn->nij/transpose | solution.py:30
  422.9 1093.1 %all-reduce.2 = bf16[6144,1,512]{2,1,0:T(2,128)(2,1)} all-reduce(f32[6144,1,512]{2,1,0:T(1,128)} %copy.8), channel_id=2, replica_groups=mesh['pair'=32,'occ'=8] {'pair'}, use_global_device_ids=true, to_apply=%region_0.1.clone | all-reduce | flops 3145728 | bytes 18874368
  1516.1 1.4 dynamic-slice_convert_fusion
  1517.5 0.7 copy.9
  1518.2 0.0 all-gather.2.cloned.1.call-update
  1518.2 55.0 %all-gather.2.cloned.1.call-done = bf16[6144,1,512]{2,0,1:T(8,128)(2,1)} async-done(((bf16[192,1,512]{2,0,1:T(8,128)(2,1)}), bf16[6144,1,512]{2,0,1:T(8,128)(2,1)}) %all-gather.2.cloned.1.call-update) | async-done | bytes 6291472 | tf_op jit(solution)/shard_map/all_gather | solution.py:38
  1573.2 0.0 copy-done
  1573.2 4.7 fusion.6
  (4 shorter events, 0.0 us)
Async XLA Ops:
  6.5 1566.7 %copy-start = (bf16[176,6144]{1,0:T(8,128)(2,1)S(1)}, bf16[176,6144]{1,0:T(8,128)(2,1)}, u32[]{:S(2)}) copy-start(bf16[176,6144]{1,0:T(8,128)(2,1)} %param.7) | copy-start | bytes 6488068
  14.3 9.2 copy-start.2
  14.3 9.2 copy-start.1
  14.3 9.5 copy-start.3
  14.3 286.5 %all-to-all-start = ((bf16[8,64,12288]{2,1,0:T(8,128)(2,1)}), bf16[8,64,12288]{2,1,0:T(8,128)(2,1)}, u32[]{:S(2)}, u32[]{:S(2)}) async-start(bf16[8,64,12288]{2,1,0:T(8,128)(2,1)} %stack.2), calls=%async_computation | async-start | bytes 25165824 | tf_op jit(solution)/shard_map/all_to_all | solution.py:7
  23.4 1549.8 %all-gather.2.cloned.1.call-start = ((), (), s32[]{:S(2)}) async-start(), calls=%async_computation.1 | async-start | bytes 6488064 | tf_op jit(solution)/shard_map/all_gather | solution.py:38
Sparse Core Ops, SparseCore 0:
  1518.3 54.8 all-gather.1
